TPU v7x, 32 devices: a whole 2x2x4 slice. The times are simulated.
32 devices in a mesh: dp: 8 (over z, y), chan: 4 (over x, core).
Axes of the slice: x: 2, y: 2, z: 4, core: 2. Of those that a mesh axis runs over, the one named last changes fastest.
Arguments:
- hidden_in: bfloat16 [768, 32768], P('chan', 'dp'), may hold values from -6 to 6
- lengths_short: int32 [128], P('dp'), may hold values from 32 to 128, as said below
- lengths_long: int32 [32], P('dp'), may hold values from 128 to 512, as said below
- qkv_weight: bfloat16 [4, 192, 576], P('chan'), may hold values from -0.4375 to 0.4375
- qv_bias: float32 [4, 384], P('chan'), may hold values from -1.75 to 1.75
- out_weight: bfloat16 [768, 768], P('chan'), may hold values from -2 to 2
- mixer_bias: float32 [768], replicated, may hold values from -3 to 3
- first_gain: float32 [768], replicated, may hold values from 0.5 to 1.5
- first_shift: float32 [768], replicated, may hold values from -3 to 3
- up_weight: bfloat16 [192, 3072], P(None, 'chan'), may hold values from -0.4375 to 0.4375
- up_bias: float32 [3072], P('chan'), may hold values from -1.75 to 1.75
- down_weight: bfloat16 [192, 3072], P(None, 'chan'), may hold values from -0.21875 to 0.21875
- down_bias: float32 [768], replicated, may hold values from -3 to 3
- second_gain: float32 [768], replicated, may hold values from 0.5 to 1.5
- second_shift: float32 [768], replicated, may hold values from -3 to 3
- out_grad: bfloat16 [32768, 768], P(('dp', 'chan')), may hold values from -6 to 6
Outputs:
- layer_out: bfloat16 [32768, 768], P(('dp', 'chan'))
- grad_input: float32 [768, 32768], P('chan', 'dp')
- grad_qkv_weight: float32 [4, 192, 576], P('chan', None, 'dp')
- grad_qv_bias: float32 [4, 384], P('chan')
- grad_out_weight: float32 [768, 768], P('chan', 'dp')
- grad_mixer_bias: float32 [768], P(('dp', 'chan'))
- grad_first_gain: float32 [768], P(('dp', 'chan'))
- grad_first_shift: float32 [768], P(('dp', 'chan'))
- grad_up_weight: float32 [192, 3072], P('dp', 'chan')
- grad_up_bias: float32 [3072], P('chan')
- grad_down_weight: float32 [192, 3072], P('dp', 'chan')
- grad_down_bias: float32 [768], P(('dp', 'chan'))
- grad_second_gain: float32 [768], P(('dp', 'chan'))
- grad_second_shift: float32 [768], P(('dp', 'chan'))
Inputs may be any that keep to these rules, and one draw needn't show every extreme that they name: `lengths_short`: tokens of a short sequence at positions under its length are valid keys; at least one short sequence has all 128 valid. `lengths_long`: likewise for the long sequences; at least one has all 512 valid.
All inputs are finite; a program needn't handle non-finite values.
Results may differ from a plain program's by a relative error of at most 0.017.
Values may be sent and summed in bfloat16 or wider, within the bound.
No kernel may reach another device: no remote copies, remote signals or barrier semaphores. Data moves between devices by JAX's collectives and lax.ppermute only.
A program may use at most 192 MiB of HBM per device.

v0:
```python
import jax
import jax.numpy as jnp
from jax import lax
from jax.sharding import PartitionSpec as P

HD = 64
LS = 128
LL = 512


EPSILON = 1e-06


def norm_rows(values, gain, shift):
    mean = jnp.mean(values, axis=-1, keepdims=True)
    centred = values - mean
    spread = jnp.mean(centred * centred, axis=-1, keepdims=True)
    return centred * lax.rsqrt(spread + EPSILON) * gain + shift


def gelu_exact(values):
    return jax.nn.gelu(values, approximate=False)


def masked_scores(query, keys, lengths):
    scale = query.shape[-1] ** (-0.5)
    raw = jnp.einsum("plhe,pmhe->phlm", query, keys, preferred_element_type=jnp.float32) * scale
    valid = (jnp.arange(keys.shape[1])[None, :] < lengths[:, None])[:, None, None, :]
    return jnp.where(valid, raw, -1000000000.0)


def attend_forward(query, keys, values, lengths):
    scores = masked_scores(query, keys, lengths)
    total = jax.nn.logsumexp(scores, axis=-1, keepdims=True)
    probs = jnp.exp(scores - total).astype(jnp.bfloat16)
    context = jnp.einsum("phlm,pmhe->plhe", probs, values, preferred_element_type=jnp.float32)
    return (context.astype(jnp.bfloat16), total)


def attend_backward(query, keys, values, lengths, total, grad_context):
    scale = query.shape[-1] ** (-0.5)
    probs = jnp.exp(masked_scores(query, keys, lengths) - total)
    grad_probs = jnp.einsum(
        "plhe,pmhe->phlm", grad_context, values, preferred_element_type=jnp.float32
    )
    inner = jnp.sum(probs * grad_probs, axis=-1, keepdims=True)
    grad_scores = (probs * (grad_probs - inner)).astype(jnp.bfloat16)
    grad_query = (
        jnp.einsum("phlm,pmhe->plhe", grad_scores, keys, preferred_element_type=jnp.float32) * scale
    )
    grad_keys = (
        jnp.einsum("phlm,plhe->pmhe", grad_scores, query, preferred_element_type=jnp.float32)
        * scale
    )
    grad_values = jnp.einsum(
        "phlm,plhe->pmhe",
        probs.astype(jnp.bfloat16),
        grad_context,
        preferred_element_type=jnp.float32,
    )
    return (
        grad_query.astype(jnp.bfloat16),
        grad_keys.astype(jnp.bfloat16),
        grad_values.astype(jnp.bfloat16),
    )


def by_blocks(function, arrays, per_block):
    count = arrays[0].shape[0]
    blocks = count // per_block
    shaped = tuple((a.reshape((blocks, per_block) + a.shape[1:]) for a in arrays))
    results = lax.map(lambda item: function(*item), shaped)
    return tuple((r.reshape((count,) + r.shape[2:]) for r in results))


def on_device(
    hidden_in,
    lengths_short,
    lengths_long,
    qkv_weight,
    qv_bias,
    out_weight,
    mixer_bias,
    first_gain,
    first_shift,
    up_weight,
    up_bias,
    down_weight,
    down_bias,
    second_gain,
    second_shift,
    out_grad,
):
    width, tokens = hidden_in.shape
    chan_count = lax.axis_size("chan")
    model = chan_count * width
    local_cols = up_weight.shape[1]
    units = local_cols // chan_count
    head_count = width // HD
    quarter = tokens // chan_count
    chan_index = lax.axis_index("chan")
    short_count = lengths_short.shape[0]
    long_count = lengths_long.shape[0]
    short_rows = short_count * LS
    bias_row = jnp.concatenate(
        [qv_bias[0, :width], jnp.zeros((width,), jnp.float32), qv_bias[0, width:]]
    )
    projected = (
        lax.dot_general(
            hidden_in, qkv_weight[0], (((0,), (0,)), ((), ())), preferred_element_type=jnp.float32
        )
        + bias_row
    ).astype(jnp.bfloat16)

    def kinds(values):
        tail = values.shape[1:]
        return (
            values[:short_rows].reshape((short_count, LS) + tail),
            values[short_rows:].reshape((long_count, LL) + tail),
        )

    query_short, query_long = kinds(projected[:, :width].reshape(tokens, head_count, HD))
    keys_short, keys_long = kinds(projected[:, width : 2 * width].reshape(tokens, head_count, HD))
    values_short, values_long = kinds(projected[:, 2 * width :].reshape(tokens, head_count, HD))
    ctx_short, total_short = by_blocks(
        attend_forward, (query_short, keys_short, values_short, lengths_short), 4
    )
    ctx_long, total_long = by_blocks(
        attend_forward, (query_long, keys_long, values_long, lengths_long), 1
    )
    context = jnp.concatenate(
        [ctx_short.reshape(short_rows, width), ctx_long.reshape(tokens - short_rows, width)], axis=0
    )
    ctx_rows = context
    own_rows = hidden_in.astype(jnp.float32).T
    term = jnp.dot(ctx_rows, out_weight, preferred_element_type=jnp.float32)
    mine = lax.dynamic_slice_in_dim(term, chan_index * width, width, 1) + own_rows
    pre_first = (
        lax.psum_scatter(
            lax.dynamic_update_slice_in_dim(term, mine, chan_index * width, 1).astype(jnp.bfloat16),
            "chan",
            scatter_dimension=0,
            tiled=True,
        ).astype(jnp.float32)
        + mixer_bias
    )
    normed, norm1_back = jax.vjp(norm_rows, pre_first, first_gain, first_shift)
    normed_low = normed.astype(jnp.bfloat16)
    up_three = up_weight.reshape(width, chan_count, units)
    down_three = down_weight.reshape(width, chan_count, units)
    rows_all = lax.all_gather(normed_low, "chan", axis=0, tiled=True)
    pre_act = jnp.einsum(
        "tgi,igh->tgh",
        rows_all.reshape(tokens, chan_count, width),
        up_three,
        preferred_element_type=jnp.float32,
    ) + up_bias.reshape(chan_count, units)
    activated = gelu_exact(pre_act).astype(jnp.bfloat16)
    act_rows = activated
    pre_second = (
        normed
        + lax.psum_scatter(
            jnp.einsum("tgh,kgh->tgk", act_rows, down_three, preferred_element_type=jnp.float32)
            .reshape(quarter * lax.axis_size("chan"), model)
            .astype(jnp.bfloat16),
            "chan",
            scatter_dimension=0,
            tiled=True,
        ).astype(jnp.float32)
        + down_bias
    )
    result, norm2_back = jax.vjp(norm_rows, pre_second, second_gain, second_shift)
    grad_second, grad_gain2, grad_shift2 = norm2_back(out_grad.astype(jnp.float32))
    grad_downb = jnp.sum(grad_second, axis=0)
    grad_down_low = grad_second.astype(jnp.bfloat16)
    piece = lax.all_gather(grad_down_low, "chan", axis=0, tiled=True)
    count = piece.shape[0]
    split_rows = piece.reshape(count, chan_count, width)
    act_rows = activated
    grad_act = jnp.einsum(
        "tgk,kgh->tgh", split_rows, down_three, preferred_element_type=jnp.float32
    )
    grad_rows = jax.vjp(gelu_exact, pre_act)[1](grad_act)[0].astype(jnp.bfloat16)
    down_total = jnp.einsum(
        "tgh,tgk->kgh", act_rows, split_rows, preferred_element_type=jnp.float32
    )
    grad_buffer = grad_rows
    grad_down = down_total
    grad_down = grad_down.reshape(width, local_cols)
    grad_up = jnp.einsum(
        "tgi,tgh->igh",
        rows_all.reshape(tokens, chan_count, width),
        grad_buffer,
        preferred_element_type=jnp.float32,
    ).reshape(width, local_cols)
    grad_upb = jnp.sum(grad_buffer, axis=0, dtype=jnp.float32).reshape(local_cols)
    grad_rows = grad_buffer
    grad_normed = (
        lax.psum_scatter(
            jnp.einsum("tgh,igh->tgi", grad_rows, up_three, preferred_element_type=jnp.float32)
            .reshape(quarter * lax.axis_size("chan"), model)
            .astype(jnp.bfloat16),
            "chan",
            scatter_dimension=0,
            tiled=True,
        ).astype(jnp.float32)
        + grad_second
    )
    grad_first, grad_gain1, grad_shift1 = norm1_back(grad_normed)
    grad_first_low = grad_first.astype(jnp.bfloat16)
    grad_mixer = jnp.sum(grad_first_low, axis=0, dtype=jnp.float32)
    piece = lax.all_gather(grad_first_low, "chan", axis=0, tiled=True)
    ctx_rows = context
    out_total = lax.dot_general(
        ctx_rows, piece, (((0,), (0,)), ((), ())), preferred_element_type=jnp.float32
    )
    rows_grad = lax.dot_general(
        piece, out_weight, (((1,), (1,)), ((), ())), preferred_element_type=jnp.float32
    ).astype(jnp.bfloat16)
    own_rows = lax.dynamic_slice_in_dim(piece, chan_index * width, width, 1)
    through = own_rows.T
    local_out, grad_context, through = (out_total, rows_grad, through)
    back_short, back_long = kinds(grad_context.reshape(tokens, head_count, HD))
    grads_short = by_blocks(
        attend_backward,
        (query_short, keys_short, values_short, lengths_short, total_short, back_short),
        4,
    )
    grads_long = by_blocks(
        attend_backward,
        (query_long, keys_long, values_long, lengths_long, total_long, back_long),
        1,
    )

    def joined(index):
        return jnp.concatenate(
            [
                grads_short[index].reshape(short_rows, width),
                grads_long[index].reshape(tokens - short_rows, width),
            ],
            axis=0,
        )

    grad_projected = jnp.concatenate([joined(0), joined(1), joined(2)], axis=1)
    local_qkv = jnp.dot(hidden_in, grad_projected, preferred_element_type=jnp.float32)[None]
    column_sums = jnp.sum(grad_projected, axis=0, dtype=jnp.float32)
    local_qv = jnp.concatenate([column_sums[:width], column_sums[2 * width :]])[None]
    grad_input = lax.dot_general(
        qkv_weight[0], grad_projected, (((1,), (1,)), ((), ())), preferred_element_type=jnp.float32
    ) + through.astype(jnp.float32)
    grad_qkv, grad_out, grad_up, grad_down = (
        lax.psum_scatter(local_qkv, "dp", scatter_dimension=2, tiled=True),
        lax.psum_scatter(local_out, "dp", scatter_dimension=1, tiled=True),
        lax.psum_scatter(grad_up, "dp", scatter_dimension=0, tiled=True),
        lax.psum_scatter(grad_down, "dp", scatter_dimension=0, tiled=True),
    )
    grad_qv, grad_upb = lax.psum((local_qv, grad_upb), "dp")
    vectors = jnp.stack([grad_mixer, grad_gain1, grad_shift1, grad_downb, grad_gain2, grad_shift2])
    vectors = lax.psum_scatter(vectors, ("dp", "chan"), scatter_dimension=1, tiled=True)
    return (
        result.astype(jnp.bfloat16),
        grad_input,
        grad_qkv,
        grad_qv,
        grad_out,
        vectors[0],
        vectors[1],
        vectors[2],
        grad_up,
        grad_upb,
        grad_down,
        vectors[3],
        vectors[4],
        vectors[5],
    )


def solution(mesh):
    in_specs = (
        P("chan", "dp"),
        P("dp"),
        P("dp"),
        P("chan", None, None),
        P("chan", None),
        P("chan", None),
        P(),
        P(),
        P(),
        P(None, "chan"),
        P("chan"),
        P(None, "chan"),
        P(),
        P(),
        P(),
        P(("dp", "chan"), None),
    )
    out_specs = (
        P(("dp", "chan"), None),
        P("chan", "dp"),
        P("chan", None, "dp"),
        P("chan", None),
        P("chan", "dp"),
        P(("dp", "chan")),
        P(("dp", "chan")),
        P(("dp", "chan")),
        P("dp", "chan"),
        P("chan"),
        P("dp", "chan"),
        P(("dp", "chan")),
        P(("dp", "chan")),
        P(("dp", "chan")),
    )
    return jax.shard_map(
        on_device, mesh=mesh, in_specs=in_specs, out_specs=out_specs, check_vma=False
    )
```

profile of v0, /device:TPU:0, one launch (start us, length us, event | category | flops | bytes accessed | tf_op | source)
XLA Modules:
  0.0 876.1 jit_solution(13439938410316223014)
XLA Ops:
  21.9 19.8 %while.53 = (s32[]{:T(128)}, bf16[4,1,512,3,64]{2,4,3,1,0:T(8,128)(2,1)}, f32[4,1,3,512,1]{3,2,4,1,0:T(4,128)}, bf16[4,1,512,3,64]{2,4,3,1,0:T(8,128)(2,1)S(1)},...) while((s32[]{:T(128)}, ...), condition=%wide.region_7.8_spmd, body=%wide.region_4.7_spmd.sunk | while | flops 210088448 | bytes 10306149 | solution.py:72
  56.5 11.9 %while.52 = (s32[]{:T(128)}, bf16[4,4,128,3,64]{2,1,0,4,3:T(4,128)(2,1)}, f32[4,4,3,128,1]{3,2,1,4,0:T(4,128)}, bf16[4,4,128,3,64]{2,4,3,1,0:T(8,128)(2,1)S(1)},...) while((s32[]{:T(128)}, ...), condition=%wide.region_3.4_spmd, body=%wide.region_0.3_spmd.sunk | while | flops 51819008 | bytes 3619981 | solution.py:72
  74.3 7.8 fusion.146
  86.5 8.1 convert_element_type.153
  94.9 60.6 %reduce-scatter.10.cloned.1.call-done = bf16[1024,768]{0,1:T(8,128)(2,1)} async-done(((bf16[4096,768]{0,1:T(8,128)(2,1)}), bf16[1024,768]{0,1:T(8,128)(2,1)}) %reduce-scatter.10.cloned.1.call-update) | async-done | bytes 1572880 | tf_op jit(solution)/shard_map/reduce_scatter | solution.py:139
  162.2 45.8 %all-gather.4.cloned.1.call-done = bf16[4096,768]{0,1:T(8,128)(2,1)} async-done(((bf16[1024,768]{0,1:T(8,128)(2,1)}), bf16[4096,768]{0,1:T(8,128)(2,1)}) %all-gather.4.cloned.1.call-update) | async-done | bytes 6291472 | tf_op jit(solution)/shard_map/all_gather | solution.py:151
  208.0 32.3 %fusion.106 = (bf16[4096,4,192]{0,2,1:T(8,128)(2,1)S(1)}, f32[4096,4,192]{0,2,1:T(8,128)}, f32[4,4096,192]{1,2,0:T(8,128)}) fusion(f32[4,192]{1,0:T(4,128)S(1)} %add.166, bf16[4096,4,192]{0,2,1:T(8,128)(2,1)} %bitcast.435, bf16[192,4,192]{2,1,0:T(4,128)(2,1)S(1)} %reshape.408), kind=kOutput, calls=%fused_computation.148 | convolution fusion | flops 1415577600 | bytes 38046720 | tf_op jit(solution)/shard_map/tgi,igh->tgh/dot_general | solution.py:152
  247.1 55.9 %reduce-scatter.12.cloned.1.call-done = bf16[1024,768]{0,1:T(8,128)(2,1)} async-done(((bf16[4096,768]{0,1:T(8,128)(2,1)}), bf16[1024,768]{0,1:T(8,128)(2,1)}) %reduce-scatter.12.cloned.1.call-update) | async-done | bytes 1572880 | tf_op jit(solution)/shard_map/reduce_scatter | solution.py:162
  313.4 46.5 %all-gather.6.cloned.1.call-done = bf16[4096,768]{0,1:T(8,128)(2,1)} async-done(((bf16[1024,768]{0,1:T(8,128)(2,1)}), bf16[4096,768]{0,1:T(8,128)(2,1)}) %all-gather.6.cloned.1.call-update) | async-done | bytes 6291472 | tf_op jit(solution)/shard_map/all_gather | solution.py:176
  359.9 13.6 %convert_reduce_fusion = (f32[4,192]{1,0:T(4,128)S(1)}, bf16[4096,4,192]{0,2,1:T(8,128)(2,1)S(1)}) fusion(f32[4096,4,192]{0,2,1:T(8,128)} %get-tuple-element.440, bf16[192,4,192]{0,2,1:T(8,128)(2,1)S(1)} %bitcast.429, bf16[4096,4,192]{0,2,1:T(8,128)(2,1)} %bitcast.437, f32[4,4096,192]{1,2,0:T(8,128)} %get-tuple-element.470, f32[4,192]{1,0:T(4,128)S(1)} %add.166), kind=kOutput, calls=%fused_computation.149 | convolution fusion | flops 1261436160 | bytes 38049792 | tf_op jit(solution)/shard_map/tgk,kgh->tgh/dot_general | solution.py:180
  378.2 57.8 %reduce-scatter.14.cloned.1.call-done = bf16[1024,768]{0,1:T(8,128)(2,1)} async-done(((bf16[4096,768]{0,1:T(8,128)(2,1)}), bf16[1024,768]{0,1:T(8,128)(2,1)}) %reduce-scatter.14.cloned.1.call-update) | async-done | bytes 1572880 | tf_op jit(solution)/shard_map/reduce_scatter | solution.py:199
  442.7 46.5 %all-gather.8.cloned.1.call-done = bf16[4096,768]{0,1:T(8,128)(2,1)} async-done(((bf16[1024,768]{0,1:T(8,128)(2,1)}), bf16[4096,768]{0,1:T(8,128)(2,1)}) %all-gather.8.cloned.1.call-update) | async-done | bytes 6291472 | tf_op jit(solution)/shard_map/all_gather | solution.py:212
  497.4 22.8 %while.54 = (s32[]{:T(128)}, bf16[4,4,128,3,64]{2,1,0,4,3:T(4,128)(2,1)S(1)}, bf16[4,4,128,3,64]{2,1,0,4,3:T(4,128)(2,1)}, bf16[4,4,128,3,64]{2,1,0,4,3:T(4,128)...) while((s32[]{:T(128)}, ...), condition=%wide.region_21.22_spmd, body=%wide.region_19.21_spmd.sunk | while | flops 128089088 | bytes 9473205 | solution.py:72
  532.4 36.3 %while.55 = (s32[]{:T(128)}, bf16[4,1,512,3,64]{2,4,3,1,0:T(8,128)(2,1)}, bf16[4,1,512,3,64]{2,4,3,1,0:T(8,128)(2,1)}, bf16[4,1,512,3,64]{2,4,3,1,0:T(8,128)(2,1...) while((s32[]{:T(128)}, ...), condition=%wide.region_24.25_spmd, body=%wide.region_22.24_spmd.sunk | while | flops 510884864 | bytes 25598080 | solution.py:72
  573.5 20.2 %convert_reduce_fusion.1 = (f32[576]{0:T(1024)S(1)}, bf16[4096,576]{0,1:T(8,128)(2,1)S(1)}) fusion(bf16[2048,192]{0,1:T(8,128)(2,1)S(1)} %bitcast.422, bf16[2048,192]{0,1:T(8,128)(2,1)S(1)} %copy-done.21, bf16[2048,192]{0,1:T(8,128)(2,1)S(1)} %bitcast.421, bf16[2048,192]{0,1:T(8,128)(2,1)S(1)} %copy-done.20, bf16[2048,192]{0,1:T(8,128)(2,1)S(1)} %bitcast.420, ...), kind=kLoop, calls=%fused_computation.163 | loop fusion | flops 33029568 | bytes 9439488 | tf_op jit(solution)/shard_map/reduce_sum | solution.py:246
  598.9 5.5 convolution_bitcast_fusion
  604.5 6.5 fusion.148
  615.3 6.5 fusion.147
  623.0 39.7 %all-reduce.1 = f32[6,768]{1,0:T(8,128)S(1)} all-reduce(f32[6,768]{1,0:T(8,128)S(1)} %stack.15), channel_id=7, replica_groups=mesh['dp'=8,'chan'=4] {'dp','chan'}, use_global_device_ids=true, to_apply=%region_35.36.clone | all-reduce | flops 4608 | bytes 36864
  663.5 22.2 %all-reduce.2 = (f32[1,384]{1,0:T(1,128)}, f32[768]{0:T(1024)}) all-reduce(f32[1,384]{1,0:T(1,128)S(1)} %broadcast_in_dim.134, f32[768]{0:T(1024)S(1)} %reshape.416), channel_id=1, replica_groups=mesh['dp'=8,'chan'=4] {'dp'}, use_global_device_ids=true, to_apply=%region_27.28 | all-reduce | flops 1152 | bytes 9216 | tf_op jit(solution)/shard_map/psum | solution.py:257
  685.7 5.9 fusion.119
  693.1 44.8 %reduce-scatter.20.cloned.1.call-done = f32[96,192]{1,0:T(8,128)} async-done(((f32[768,192]{1,0:T(8,128)}), f32[96,192]{1,0:T(8,128)}) %reduce-scatter.20.cloned.1.call-update) | async-done | bytes 73744
  739.5 64.0 %reduce-scatter.18.cloned.1.call-done = f32[24,768]{1,0:T(8,128)} async-done(((f32[192,768]{1,0:T(8,128)}), f32[24,768]{1,0:T(8,128)}) %reduce-scatter.18.cloned.1.call-update) | async-done | bytes 73744 | tf_op jit(solution)/shard_map/reduce_scatter | solution.py:255
  803.5 65.5 %reduce-scatter.16.cloned.1.call-done = f32[24,768]{1,0:T(8,128)} async-done(((f32[192,768]{1,0:T(8,128)}), f32[24,768]{1,0:T(8,128)}) %reduce-scatter.16.cloned.1.call-update) | async-done | bytes 73744 | tf_op jit(solution)/shard_map/reduce_scatter | solution.py:254
  (360 shorter events, 204.1 us)
Async XLA Ops:
  7.2 67.1 %copy-start = (bf16[192,768]{1,0:T(8,128)(2,1)S(1)}, bf16[192,768]{1,0:T(8,128)(2,1)}, u32[]{:S(2)}) copy-start(bf16[192,768]{1,0:T(8,128)(2,1)} %param.29) | copy-start | bytes 884740
  7.2 148.3 %reduce-scatter.10.cloned.1.call-start = ((), (), s32[]{:S(2)}) async-start(), calls=%async_computation.6 | async-start | bytes 7864320 | tf_op jit(solution)/shard_map/reduce_scatter | solution.py:139
  68.4 13.6 %copy-start.9 = (bf16[4,4,128,3,64]{2,4,3,1,0:T(8,128)(2,1)}, bf16[4,4,128,3,64]{2,4,3,1,0:T(8,128)(2,1)S(1)}, u32[]{:S(2)}) copy-start(bf16[4,4,128,3,64]{2,4,3,1,0:T(8,128)(2,1)S(1)} %get-tuple-element.834) | copy-start | bytes 2359300
  68.4 13.6 %copy-start.11 = (bf16[4,4,128,3,64]{2,4,3,1,0:T(8,128)(2,1)}, bf16[4,4,128,3,64]{2,4,3,1,0:T(8,128)(2,1)S(1)}, u32[]{:S(2)}) copy-start(bf16[4,4,128,3,64]{2,4,3,1,0:T(8,128)(2,1)S(1)} %get-tuple-element.835) | copy-start | bytes 2359300
  68.4 13.6 %copy-start.13 = (bf16[4,4,128,3,64]{2,4,3,1,0:T(8,128)(2,1)}, bf16[4,4,128,3,64]{2,4,3,1,0:T(8,128)(2,1)S(1)}, u32[]{:S(2)}) copy-start(bf16[4,4,128,3,64]{2,4,3,1,0:T(8,128)(2,1)S(1)} %get-tuple-element.836) | copy-start | bytes 2359300
  94.6 60.9 %copy-start.35 = (f32[768]{0:T(1024)S(1)}, f32[768]{0:T(1024)}, u32[]{:S(2)}) copy-start(f32[768]{0:T(1024)} %param.30) | copy-start | bytes 9220
  94.6 64.9 %copy-start.36 = (f32[768]{0:T(1024)S(1)}, f32[768]{0:T(1024)}, u32[]{:S(2)}) copy-start(f32[768]{0:T(1024)} %param.31) | copy-start | bytes 9220
  94.7 64.9 %copy-start.38 = (f32[768]{0:T(1024)S(1)}, f32[768]{0:T(1024)}, u32[]{:S(2)}) copy-start(f32[768]{0:T(1024)} %param.32) | copy-start | bytes 9220
  94.7 113.3 %all-gather.4.cloned.1.call-start = ((), (), s32[]{:S(2)}) async-start(), calls=%async_computation.7 | async-start | bytes 7864320 | tf_op jit(solution)/shard_map/all_gather | solution.py:151
  161.5 141.5 %reduce-scatter.12.cloned.1.call-start = ((), (), s32[]{:S(2)}) async-start(), calls=%async_computation.8 | async-start | bytes 7864320 | tf_op jit(solution)/shard_map/reduce_scatter | solution.py:162
  161.9 78.4 %copy-start.27 = (bf16[192,4,192]{2,1,0:T(4,128)(2,1)}, bf16[192,4,192]{2,1,0:T(4,128)(2,1)S(1)}, u32[]{:S(2)}) copy-start(bf16[192,4,192]{2,1,0:T(4,128)(2,1)S(1)} %reshape.408) | copy-start | bytes 884740
  162.2 78.1 %copy-start.29 = (bf16[192,768]{0,1:T(8,128)(2,1)}, bf16[192,768]{0,1:T(8,128)(2,1)S(1)}, u32[]{:S(2)}) copy-start(bf16[192,768]{0,1:T(8,128)(2,1)S(1)} %copy.161) | copy-start | bytes 884740
  244.9 58.0 %copy-start.41 = (f32[768]{0:T(1024)S(1)}, f32[768]{0:T(1024)}, u32[]{:S(2)}) copy-start(f32[768]{0:T(1024)} %param.36) | copy-start | bytes 9220
  244.9 115.0 %all-gather.6.cloned.1.call-start = ((), (), s32[]{:S(2)}) async-start(), calls=%async_computation.9 | async-start | bytes 7864320 | tf_op jit(solution)/shard_map/all_gather | solution.py:176
  311.8 48.1 %copy-start.30 = (bf16[192,768]{0,1:T(8,128)(2,1)S(1)}, bf16[192,768]{0,1:T(8,128)(2,1)}, u32[]{:S(2)}) copy-start(bf16[192,768]{0,1:T(8,128)(2,1)} %copy-done.29) | copy-start | bytes 884740
  313.4 122.7 %reduce-scatter.14.cloned.1.call-start = ((), (), s32[]{:S(2)}) async-start(), calls=%async_computation.10 | async-start | bytes 7864320 | tf_op jit(solution)/shard_map/reduce_scatter | solution.py:199
  359.9 13.6 %copy-start.28 = (bf16[192,4,192]{2,1,0:T(4,128)(2,1)S(1)}, bf16[192,4,192]{2,1,0:T(4,128)(2,1)}, u32[]{:S(2)}) copy-start(bf16[192,4,192]{2,1,0:T(4,128)(2,1)} %copy-done.27) | copy-start | bytes 884740
  378.0 111.1 %all-gather.8.cloned.1.call-start = ((), (), s32[]{:S(2)}) async-start(), calls=%async_computation.11 | async-start | bytes 7864320 | tf_op jit(solution)/shard_map/all_gather | solution.py:212
  442.7 248.9 %all-reduce.5.cloned.1.call-start = ((), (), s32[]{:S(2)}) async-start(), calls=%async_computation.15 | async-start | bytes 1179648
  573.5 22.3 %copy-start.31 = (bf16[192,4096]{1,0:T(8,128)(2,1)S(1)}, bf16[192,4096]{1,0:T(8,128)(2,1)}, u32[]{:S(2)}) copy-start(bf16[192,4096]{1,0:T(8,128)(2,1)} %param.24) | copy-start | bytes 4718596
  598.9 139.0 %reduce-scatter.20.cloned.1.call-start = ((), (), s32[]{:S(2)}) async-start(), calls=%async_computation.14 | async-start | bytes 884736
  604.5 199.0 %reduce-scatter.18.cloned.1.call-start = ((), (), s32[]{:S(2)}) async-start(), calls=%async_computation.13 | async-start | bytes 663552 | tf_op jit(solution)/shard_map/reduce_scatter | solution.py:255
  612.1 256.8 %reduce-scatter.16.cloned.1.call-start = ((), (), s32[]{:S(2)}) async-start(), calls=%async_computation.12 | async-start | bytes 663552 | tf_op jit(solution)/shard_map/reduce_scatter | solution.py:254
  615.3 70.3 %copy-start.34 = (bf16[1,192,576]{2,1,0:T(8,128)(2,1)S(1)}, bf16[1,192,576]{2,1,0:T(8,128)(2,1)}, u32[]{:S(2)}) copy-start(bf16[1,192,576]{2,1,0:T(8,128)(2,1)} %param.27) | copy-start | bytes 663556
  (32 other events, 137.1 us)
Sparse Core Ops, SparseCore 0:
  94.8 60.6 reduce-scatter.9
  161.6 46.3 all-gather.3
  245.0 57.8 reduce-scatter.11
  313.5 46.3 all-gather.5
  378.1 57.8 reduce-scatter.13
  442.8 46.3 all-gather.7
  599.0 73.2 all-reduce.4
  675.6 62.2 reduce-scatter.19
  741.7 61.7 reduce-scatter.17
  807.2 61.7 reduce-scatter.15
where the time goes:
time: 882 us; the launch traced here: 876 us
  waiting for transfers between devices  487 us (55%)
  matrix products  143 us (16%)
  local copies, waits for them, and re-layouts  94.1 us (11%)
  other arithmetic  71.6 us (8%)
  blocking collectives  61.9 us (7%)
  between operations  15.8 us (2%)
    reduce_scatter x1, waiting for transfers between devices, on_device(): lax.psum_scatter(grad_up, 'dp', scatter_dimension=0, tiled=True)  65.5 us
    reduce_scatter x1, waiting for transfers between devices, on_device(): lax.psum_scatter(grad_down, 'dp', scatter_dimension=0, tiled=True)  64 us
    reduce_scatter x1, waiting for transfers between devices, on_device(): lax.psum_scatter(lax.dynamic_update_slice_in_dim(term, mine, chan_index *...  60.6 us
    reduce_scatter x1, waiting for transfers between devices, on_device(): lax.psum_scatter(jnp.einsum('tgh,igh->tgi', grad_rows, up_three, preferre...  57.8 us
    reduce_scatter x1, waiting for transfers between devices, on_device(): lax.psum_scatter(jnp.einsum('tgh,kgh->tgk', act_rows, down_three, preferr...  55.9 us
    all_gather x1, waiting for transfers between devices, on_device(): piece = lax.all_gather(grad_first_low, 'chan', axis=0, tiled=True)  46.5 us
    all_gather x1, waiting for transfers between devices, on_device(): piece = lax.all_gather(grad_down_low, 'chan', axis=0, tiled=True)  46.5 us
    all_gather x1, waiting for transfers between devices, on_device(): rows_all = lax.all_gather(normed_low, 'chan', axis=0, tiled=True)  45.8 us
  transfers between devices with their start and end apart: 10, of which 9 were waited for; matrix products, arithmetic and copies ran while one was open for 4% of the time, Pallas kernels for 0%

commit v1 on v0

v1 whole, which is shorter than its diff:
```python
import functools

import jax
import jax.numpy as jnp
from jax import lax
from jax.experimental import pallas as pl
from jax.experimental.pallas import tpu as pltpu
from jax.sharding import PartitionSpec as P

HD = 64
LS = 128
LL = 512
TILE = 256
EPSILON = 1e-06
LOG2E = 1.4426950408889634
F32 = jnp.float32
BF16 = jnp.bfloat16
VMEM_LIMIT = 60 * 1024 * 1024


def dot(a, b, ca, cb):
    return lax.dot_general(a, b, (((ca,), (cb,)), ((), ())), preferred_element_type=F32)


def gelu_parts(v):
    av = jnp.abs(v)
    t = 1.0 / (1.0 + (0.3275911 * 0.7071067811865476) * av)
    e = jnp.exp2((-0.5 * LOG2E) * (v * v))
    poly = t * (
        0.5 * 0.254829592
        + t
        * (
            0.5 * -0.284496736
            + t * (0.5 * 1.421413741 + t * (0.5 * -1.453152027 + t * (0.5 * 1.061405429)))
        )
    )
    tail = poly * e
    phi = jnp.where(v >= 0, 1.0 - tail, tail)
    return phi, phi + v * (0.3989422804014327 * e)


def attn_fwd_kernel(
    half, heads, short_blocks, me, lens_s, lens_l, x, w, b, proj, ctx0, ctx1, ctx2, ctx3, lse, scr
):
    k = pl.program_id(0)
    block = lax.bitwise_xor(me[0], k) * 2 + half
    width = heads * HD
    span = x.shape[1]
    proj[0] = (dot(w[...], x[...], 0, 0) + b[...]).astype(BF16)

    def one(rows, cols, length):
        q = proj[0, rows[0], cols]
        key = proj[0, rows[1], cols]
        val = proj[0, rows[2], cols]
        s = dot(key, q, 0, 0) * (HD**-0.5 * LOG2E)
        pos = lax.broadcasted_iota(jnp.int32, s.shape, 0)
        s = jnp.where(pos < length, s, -1e9)
        m = jnp.max(s, axis=0, keepdims=True)
        e = jnp.exp2(s - m)
        total = jnp.sum(e, axis=0, keepdims=True)
        c = dot(val, e.astype(BF16), 1, 0) * (1.0 / total)
        return c.astype(BF16), m + jnp.log2(total)

    def run(seq_len, lens, first):
        for i in range(span // seq_len):
            cols = slice(i * seq_len, (i + 1) * seq_len)
            length = lens[first + i]
            for h in range(heads):
                rows = [slice(j * width + h * HD, j * width + (h + 1) * HD) for j in range(3)]
                c, total = one(rows, cols, length)
                scr[h * HD : (h + 1) * HD, cols] = c
                lse[0, h : h + 1, cols] = total

    @pl.when(block < short_blocks)
    def _():
        run(LS, lens_s, block * (span // LS))

    @pl.when(block >= short_blocks)
    def _():
        run(LL, lens_l, (block - short_blocks) * (span // LL))

    for i, out in enumerate((ctx0, ctx1, ctx2, ctx3)):

        @pl.when(k == i)
        def _():
            out[...] = scr[...]


def attn_fwd(half, me, lens_s, lens_l, x, w, b):
    width, tokens = x.shape
    span = tokens // 8
    heads = width // HD
    short_blocks = lens_s.shape[0] * LS // span
    fixed = lambda k, *_: (0, 0)
    piece = jax.ShapeDtypeStruct((width, span), BF16)
    return pl.pallas_call(
        functools.partial(attn_fwd_kernel, half, heads, short_blocks),
        grid_spec=pltpu.PrefetchScalarGridSpec(
            num_scalar_prefetch=3,
            grid=(4,),
            in_specs=[
                pl.BlockSpec(
                    (width, span), lambda k, me, *_: (0, lax.bitwise_xor(me[0], k) * 2 + half)
                ),
                pl.BlockSpec(w.shape, fixed),
                pl.BlockSpec(b.shape, fixed),
            ],
            out_specs=[
                pl.BlockSpec((1, 3 * width, span), lambda k, *_: (k, 0, 0)),
                pl.BlockSpec((width, span), fixed),
                pl.BlockSpec((width, span), fixed),
                pl.BlockSpec((width, span), fixed),
                pl.BlockSpec((width, span), fixed),
                pl.BlockSpec((1, heads, span), lambda k, *_: (k, 0, 0)),
            ],
            scratch_shapes=[pltpu.VMEM((width, span), BF16)],
        ),
        out_shape=[
            jax.ShapeDtypeStruct((4, 3 * width, span), BF16),
            piece,
            piece,
            piece,
            piece,
            jax.ShapeDtypeStruct((4, heads, span), F32),
        ],
        compiler_params=pltpu.CompilerParams(vmem_limit_bytes=VMEM_LIMIT),
        name=f"attn_fwd{half}",
    )(me, lens_s, lens_l, x, w, b)


def attn_bwd_kernel(half, heads, short_blocks, me, lens_s, lens_l, *refs):
    if half:
        (x, w, proj, lse, g0, g1, g2, g3, f0, f1, f2, f3, acc_in, bias_in, old) = refs[:15]
        gin, acc, bias, dproj, gsc, fsc = refs[15:]
    else:
        (x, w, proj, lse, g0, g1, g2, g3, f0, f1, f2, f3) = refs[:12]
        gin, acc, bias, dproj, gsc, fsc = refs[12:]
    k = pl.program_id(0)
    block = lax.bitwise_xor(me[0], k) * 2 + half
    width = heads * HD
    span = x.shape[1]
    scale = HD**-0.5
    for i, (g, f) in enumerate(((g0, f0), (g1, f1), (g2, f2), (g3, f3))):

        @pl.when(k == i)
        def _():
            gsc[...] = g[...]
            fsc[...] = f[...]

    def run(seq_len, lens, first):
        for i in range(span // seq_len):
            cols = slice(i * seq_len, (i + 1) * seq_len)
            length = lens[first + i]
            for h in range(heads):
                rq, rk, rv = [
                    slice(j * width + h * HD, j * width + (h + 1) * HD) for j in range(3)
                ]
                q = proj[0, rq, cols]
                key = proj[0, rk, cols]
                val = proj[0, rv, cols]
                go = gsc[h * HD : (h + 1) * HD, cols]
                s = dot(key, q, 0, 0) * (scale * LOG2E)
                pos = lax.broadcasted_iota(jnp.int32, s.shape, 0)
                s = jnp.where(pos < length, s, -1e9)
                p = jnp.exp2(s - lse[0, h : h + 1, cols])
                gp = dot(val, go, 0, 0)
                inner = jnp.sum(p * gp, axis=0, keepdims=True)
                gs = (p * (gp - inner)).astype(BF16)
                dproj[rq, cols] = (dot(key, gs, 1, 0) * scale).astype(BF16)
                dproj[rk, cols] = (dot(q, gs, 1, 1) * scale).astype(BF16)
                dproj[rv, cols] = dot(go, p.astype(BF16), 1, 1).astype(BF16)

    @pl.when(block < short_blocks)
    def _():
        run(LS, lens_s, block * (span // LS))

    @pl.when(block >= short_blocks)
    def _():
        run(LL, lens_l, (block - short_blocks) * (span // LL))

    gin[...] = dot(w[...], dproj[...], 1, 0) + fsc[...].astype(F32)
    part = dot(dproj[...], x[...], 1, 1)
    sums = jnp.sum(dproj[...].astype(F32), axis=1, keepdims=True)

    @pl.when(k == 0)
    def _():
        if half:
            acc[...] = acc_in[...] + part
            bias[...] = bias_in[...] + sums
        else:
            acc[...] = part
            bias[...] = sums

    @pl.when(k > 0)
    def _():
        acc[...] += part
        bias[...] += sums


def attn_bwd(half, me, lens_s, lens_l, x, w, proj, lse, g, f, carry):
    width, tokens = x.shape
    span = tokens // 8
    heads = width // HD
    short_blocks = lens_s.shape[0] * LS // span
    fixed = lambda k, *_: (0, 0)
    here = lambda k, me, *_: (0, lax.bitwise_xor(me[0], k) * 2 + half)
    piece = pl.BlockSpec((width, span), fixed)
    acc_spec = pl.BlockSpec((3 * width, width), fixed)
    bias_spec = pl.BlockSpec((3 * width, 1), fixed)
    in_specs = [
        pl.BlockSpec((width, span), here),
        pl.BlockSpec(w.shape, fixed),
        pl.BlockSpec((1, 3 * width, span), lambda k, *_: (k, 0, 0)),
        pl.BlockSpec((1, heads, span), lambda k, *_: (k, 0, 0)),
    ] + [piece] * 8
    args = [x, w, proj, lse, *g, *f]
    aliases = {}
    if half:
        gin, acc, bias = carry
        in_specs += [acc_spec, bias_spec, pl.BlockSpec(memory_space=pl.ANY)]
        args += [acc, bias, gin]
        aliases = {3 + len(args) - 1: 0}
    return pl.pallas_call(
        functools.partial(attn_bwd_kernel, half, heads, short_blocks),
        grid_spec=pltpu.PrefetchScalarGridSpec(
            num_scalar_prefetch=3,
            grid=(4,),
            in_specs=in_specs,
            out_specs=[pl.BlockSpec((width, span), here), acc_spec, bias_spec],
            scratch_shapes=[
                pltpu.VMEM((3 * width, span), BF16),
                pltpu.VMEM((width, span), BF16),
                pltpu.VMEM((width, span), BF16),
            ],
        ),
        out_shape=[
            jax.ShapeDtypeStruct((width, tokens), F32),
            jax.ShapeDtypeStruct((3 * width, width), F32),
            jax.ShapeDtypeStruct((3 * width, 1), F32),
        ],
        input_output_aliases=aliases,
        compiler_params=pltpu.CompilerParams(vmem_limit_bytes=VMEM_LIMIT),
        name=f"attn_bwd{half}",
    )(me, lens_s, lens_l, *args)


def mid_kernel(half, width, me, *refs):
    ctx, hid = refs[0:4], refs[4:8]
    og = refs[8]
    ow, up, dn = refs[9:13], refs[13:17], refs[17:21]
    cols, ub = refs[21], refs[22]
    at = 23
    if half:
        gow_in, gup_in, gdn_in, vec_in = refs[at : at + 4]
        at += 4
    lo = refs[at]
    gctx, gpf_out = refs[at + 1 : at + 5], refs[at + 5 : at + 9]
    gow, gup, gdn, vec = refs[at + 9 : at + 13]
    upt, dnt, act, slope, first, n1s, gps_s = refs[at + 13 :]
    step = pl.program_id(0)
    model = 4 * width
    inv = 1.0 / model

    @pl.when(step == 0)
    def _():
        for k in range(4):
            ut = up[k][...].T
            dt = dn[k][...].T
            for g in range(4):
                upt[g, k * width : (k + 1) * width, :] = ut[g * width : (g + 1) * width, :]
                dnt[g, k * width : (k + 1) * width, :] = dt[g * width : (g + 1) * width, :]
        if half:
            gow[...] = gow_in[...]
            gup[...] = gup_in[...]
            gdn[...] = gdn_in[...]
            vec[...] = vec_in[...]
        else:
            gow[...] = jnp.zeros_like(gow)
            gup[...] = jnp.zeros_like(gup)
            gdn[...] = jnp.zeros_like(gdn)
            vec[...] = jnp.zeros_like(vec)

    def col(j):
        return cols[:, j : j + 1]

    lane = lax.broadcasted_iota(jnp.int32, (1, vec.shape[1]), 1)

    def add_vec(j, value):
        vec[...] += jnp.where(lane == j, jnp.sum(value, axis=1, keepdims=True), 0.0)

    first[...] = col(0) + sum(dot(ow[k][...], ctx[k][...], 0, 0) for k in range(4))
    for k in range(4):
        rows = pl.ds(pl.multiple_of(lax.bitwise_xor(me[0], k) * width, width), width)
        first[rows, :] += hid[k][...].astype(F32)
    pre = first[...]
    cen = pre - jnp.sum(pre, axis=0, keepdims=True) * inv
    r1 = lax.rsqrt(jnp.sum(cen * cen, axis=0, keepdims=True) * inv + EPSILON)
    n1 = cen * r1
    n1s[...] = n1
    normed = n1 * col(1) + col(2)
    low = normed.astype(BF16)
    for g in range(4):
        rows = slice(g * width, (g + 1) * width)
        branch = jnp.zeros((width, TILE), F32)
        for k in range(4):
            units = slice(k * width, (k + 1) * width)
            pa = dot(upt[g, units, :], low[rows, :], 1, 0) + ub[rows, k : k + 1]
            phi, sl = gelu_parts(pa)
            a = (pa * phi).astype(BF16)
            act[g, units, :] = a
            slope[g, units, :] = sl
            branch += dot(dnt[g, units, :], a, 0, 0)
        first[rows, :] = normed[rows, :] + branch + cols[rows, 3:4]
    pre = first[...]
    cen = pre - jnp.sum(pre, axis=0, keepdims=True) * inv
    r2 = lax.rsqrt(jnp.sum(cen * cen, axis=0, keepdims=True) * inv + EPSILON)
    n2 = cen * r2
    lo[...] = (n2 * col(4) + col(5)).T.astype(BF16)
    ogt = og[...].astype(F32).T
    add_vec(4, ogt * n2)
    add_vec(5, ogt)
    u = ogt * col(4)
    gps = r2 * (
        u
        - jnp.sum(u, axis=0, keepdims=True) * inv
        - n2 * (jnp.sum(u * n2, axis=0, keepdims=True) * inv)
    )
    add_vec(3, gps)
    gdl = gps.astype(BF16)
    gps_s[...] = gps
    for g in range(4):
        rows = slice(g * width, (g + 1) * width)
        gn = gps_s[rows, :]
        gup_sum = []
        for k in range(4):
            units = slice(k * width, (k + 1) * width)
            ga = dot(dnt[g, units, :], gdl[rows, :], 1, 0) * slope[g, units, :]
            gpa = ga.astype(BF16)
            gup_sum.append(jnp.sum(gpa.astype(F32), axis=1, keepdims=True))
            gdn[g, units, :] += dot(act[g, units, :], gdl[rows, :], 1, 1)
            gup[g, units, :] += dot(gpa, low[rows, :], 1, 1)
            gn += dot(upt[g, units, :], gpa, 0, 0)
        vec[...] += jnp.where(lane == 6 + g, jnp.concatenate(gup_sum, axis=0), 0.0)
        gps_s[rows, :] = gn
    gn = gps_s[...]
    n1 = n1s[...]
    add_vec(1, gn * n1)
    add_vec(2, gn)
    u = gn * col(1)
    gpf = r1 * (
        u
        - jnp.sum(u, axis=0, keepdims=True) * inv
        - n1 * (jnp.sum(u * n1, axis=0, keepdims=True) * inv)
    )
    gpl = gpf.astype(BF16)
    first[...] = gpl.astype(F32)
    add_vec(0, first[...])
    for k in range(4):
        rows = pl.ds(pl.multiple_of(lax.bitwise_xor(me[0], k) * width, width), width)
        gpf_out[k][...] = first[rows, :].astype(BF16)
        gctx[k][...] = dot(ow[k][...], gpl, 1, 0).astype(BF16)
        gow[k] += dot(gpl, ctx[k][...], 1, 1)


def mid(half, me, ctx, hid, og, ow, up, dn, cols, ub, carry):
    width, span = ctx[0].shape
    model = 4 * width
    steps = span // TILE
    whole2 = lambda i, *_: (0, 0)
    whole3 = lambda i, *_: (0, 0, 0)
    tile = pl.BlockSpec((width, TILE), lambda i, *_: (0, i))
    row_in = pl.BlockSpec((TILE, model), lambda i, *_: (half * steps + i, 0))
    weight = pl.BlockSpec((width, model), whole2)
    gow_spec = pl.BlockSpec((4, model, width), whole3)
    vec_spec = pl.BlockSpec((model, 16), whole2)
    in_specs = (
        [tile] * 8
        + [row_in]
        + [weight] * 12
        + [pl.BlockSpec(cols.shape, whole2), pl.BlockSpec(ub.shape, whole2)]
    )
    args = [*ctx, *hid, og, *ow, *up, *dn, cols, ub]
    if half:
        in_specs += [gow_spec] * 3 + [vec_spec]
        args += list(carry)
    big = jax.ShapeDtypeStruct((4, model, width), F32)
    piece = jax.ShapeDtypeStruct((width, span), BF16)
    return pl.pallas_call(
        functools.partial(mid_kernel, half, width),
        grid_spec=pltpu.PrefetchScalarGridSpec(
            num_scalar_prefetch=1,
            grid=(steps,),
            in_specs=in_specs,
            out_specs=[pl.BlockSpec((TILE, model), lambda i, *_: (i, 0))]
            + [tile] * 8
            + [gow_spec] * 3
            + [vec_spec],
            scratch_shapes=[
                pltpu.VMEM((4, model, width), BF16),
                pltpu.VMEM((4, model, width), BF16),
                pltpu.VMEM((4, model, TILE), BF16),
                pltpu.VMEM((4, model, TILE), F32),
                pltpu.VMEM((model, TILE), F32),
                pltpu.VMEM((model, TILE), F32),
                pltpu.VMEM((model, TILE), F32),
            ],
        ),
        out_shape=[jax.ShapeDtypeStruct((span, model), BF16)]
        + [piece] * 8
        + [big] * 3
        + [jax.ShapeDtypeStruct((model, 16), F32)],
        compiler_params=pltpu.CompilerParams(vmem_limit_bytes=VMEM_LIMIT),
        name=f"mid{half}",
    )(me, *args)


def swap(value, axis, bit):
    count = lax.axis_size(axis)
    return lax.ppermute(value, axis, [(i, i ^ bit) for i in range(count)])


def to_chan(pieces):
    return [pieces[0]] + [swap(pieces[k], "chan", k) for k in range(1, 4)]


def gather_chan(value):
    near = swap(value, "chan", 1)
    far = swap(value, "chan", 2)
    return [value, near, far, swap(far, "chan", 1)]


def scatter_dp(pieces):
    index = lax.axis_index("dp")
    count = pieces.shape[0]
    step = 1
    while count > 1:
        part = min(8, count)
        digit = (index // step) % part
        view = pieces.reshape((count // part, part) + pieces.shape[1:])
        total = lax.dynamic_index_in_dim(view, digit, 1, keepdims=False).astype(F32)
        for e in range(1, part):
            term = lax.dynamic_index_in_dim(view, digit ^ e, 1, keepdims=False)
            total = total + swap(term, "dp", e * step).astype(F32)
        count //= part
        step *= part
        pieces = total if count == 1 else total.astype(pieces.dtype)
    return pieces[0]


def sum_dp(value):
    bit = 1
    while bit < lax.axis_size("dp"):
        value = value + swap(value, "dp", bit)
        bit *= 2
    return value


def on_device(
    hidden_in,
    lengths_short,
    lengths_long,
    qkv_weight,
    qv_bias,
    out_weight,
    mixer_bias,
    first_gain,
    first_shift,
    up_weight,
    up_bias,
    down_weight,
    down_bias,
    second_gain,
    second_shift,
    out_grad,
):
    width, tokens = hidden_in.shape
    span = tokens // 8
    model = 4 * width
    dp_count = lax.axis_size("dp")
    chan = lax.axis_index("chan").astype(jnp.int32)
    dp = lax.axis_index("dp").astype(jnp.int32)
    me = chan[None]

    def hidden_piece(k, half):
        return lax.dynamic_slice_in_dim(
            hidden_in, (lax.bitwise_xor(chan, k) * 2 + half) * span, span, 1
        )

    ow = gather_chan(out_weight)
    up = gather_chan(up_weight)
    dn = gather_chan(down_weight)
    ub = jnp.stack(gather_chan(up_bias), axis=1)
    cols = jnp.stack(
        [mixer_bias, first_gain, first_shift, down_bias, second_gain, second_shift], axis=1
    )
    bias = jnp.concatenate(
        [qv_bias[0, :width], jnp.zeros((width,), F32), qv_bias[0, width:]]
    )[:, None]
    w = qkv_weight[0]
    hid, proj, ctx, lse = [], [], [], []
    for half in range(2):
        hid.append(to_chan([hidden_piece(k, half) for k in range(4)]))
        p, c0, c1, c2, c3, total = attn_fwd(
            half, me, lengths_short, lengths_long, hidden_in, w, bias
        )
        proj.append(p)
        lse.append(total)
        ctx.append(to_chan([c0, c1, c2, c3]))
    outs, carry, gctx, gpf = [], None, [], []
    for half in range(2):
        res = mid(half, me, ctx[half], hid[half], out_grad, ow, up, dn, cols, ub, carry)
        outs.append(res[0])
        gctx.append(to_chan(res[1:5]))
        gpf.append(to_chan(res[5:9]))
        carry = res[9:13]
    gow, gup, gdn, vec = carry
    carry = None
    for half in range(2):
        carry = attn_bwd(
            half,
            me,
            lengths_short,
            lengths_long,
            hidden_in,
            w,
            proj[half],
            lse[half],
            gctx[half],
            gpf[half],
            carry,
        )
    grad_input, gqkv, gbias = carry

    def by_columns(value):
        return value.reshape(4, 4, width, width).transpose(1, 3, 0, 2).reshape(4, width, model)

    rows = jnp.concatenate([by_columns(gup), by_columns(gdn)], axis=2).astype(BF16)
    flat = gow.astype(BF16)

    def over_chan(value):
        near = value[0::2] + swap(value[1::2], "chan", 1)
        return near[0] + swap(near[1], "chan", 2)

    rows = over_chan(rows)
    flat = over_chan(flat)
    rows = scatter_dp(rows.reshape(dp_count, width // dp_count, 2 * model))
    flat = scatter_dp(flat.reshape(dp_count, model // dp_count, width))
    gq = scatter_dp(gqkv.astype(BF16).reshape(dp_count, 3 * width // dp_count, width))
    grad_qv = sum_dp(gbias[:, 0])
    vec = sum_dp(vec)
    grad_upb = over_chan(vec[:, 6:10].reshape(4, width, 4)).T.reshape(model)
    vec = vec + swap(vec, "chan", 1)
    vec = vec + swap(vec, "chan", 2)
    own = model // (4 * dp_count)
    mine = lax.dynamic_slice_in_dim(vec[:, :6], (dp * 4 + chan) * own, own, 0)
    return (
        jnp.concatenate(outs, axis=0),
        grad_input,
        gq.T[None],
        jnp.concatenate([grad_qv[:width], grad_qv[2 * width :]])[None],
        flat.T,
        mine[:, 0],
        mine[:, 1],
        mine[:, 2],
        rows[:, :model],
        grad_upb,
        rows[:, model:],
        mine[:, 3],
        mine[:, 4],
        mine[:, 5],
    )


def solution(mesh):
    in_specs = (
        P("chan", "dp"),
        P("dp"),
        P("dp"),
        P("chan", None, None),
        P("chan", None),
        P("chan", None),
        P(),
        P(),
        P(),
        P(None, "chan"),
        P("chan"),
        P(None, "chan"),
        P(),
        P(),
        P(),
        P(("dp", "chan"), None),
    )
    out_specs = (
        P(("dp", "chan"), None),
        P("chan", "dp"),
        P("chan", None, "dp"),
        P("chan", None),
        P("chan", "dp"),
        P(("dp", "chan")),
        P(("dp", "chan")),
        P(("dp", "chan")),
        P("dp", "chan"),
        P("chan"),
        P("dp", "chan"),
        P(("dp", "chan")),
        P(("dp", "chan")),
        P(("dp", "chan")),
    )
    return jax.shard_map(
        on_device, mesh=mesh, in_specs=in_specs, out_specs=out_specs, check_vma=False
    )
```

time: 882 us -> 323 us (0.37)
  waiting for transfers between devices: 487 us -> 86.3 us
  matrix products: 143 us -> 0 us
  Pallas kernels: 0 us -> 115 us
  starting transfers between devices: 1.2 us -> 69.9 us
  local copies, waits for them, and re-layouts: 94.1 us -> 30.7 us
  blocking collectives: 61.9 us -> 0 us
  other arithmetic: 71.6 us -> 13 us
  between operations: 15.8 us -> 1.7 us
    reduce_scatter x5 -> x0, waiting for transfers between devices: 304 us -> none  [the longest x1 65.5 us: on_device(): lax.psum_scatter(grad_up, 'dp', scatter_dimension=0, tiled=True)]
    all_gather x3 -> x0, waiting for transfers between devices: 139 us -> none  [the longest x1 46.5 us: on_device(): piece = lax.all_gather(grad_first_low, 'chan', axis=0, tiled=True)]
    dot_general x67 -> x0, matrix products: 138 us -> none  [the longest x1 32.3 us: on_device(): jnp.einsum('tgi,igh->tgh', rows_all.reshape(tokens, chan_count, width), u...]
    pallas_call x0 -> x6, Pallas kernels: none -> 115 us  [the longest x2 60.8 us: mid(): pl.pallas_call(functools.partial(mid_kernel, half, width), grid_spec=pltp...]
    ppermute x0 -> x71, waiting for transfers between devices: none -> 86.3 us  [swap(): return lax.ppermute(value, axis, [(i, i ^ bit) for i in range(count)])]
    ppermute x0 -> x71, starting transfers between devices: none -> 69.9 us  [swap(): return lax.ppermute(value, axis, [(i, i ^ bit) for i in range(count)])]
    unnamed x12 -> x0, waiting for transfers between devices: 44.9 us -> none
    reduce_sum x18 -> x0, other arithmetic: 40.7 us -> none  [the longest x1 20.2 us: on_device(): column_sums = jnp.sum(grad_projected, axis=0, dtype=jnp.float32)]
  transfers between devices with their start and end apart: 10 -> 71, of which waited for: 9 -> 18; matrix products, arithmetic and copies ran while one was open for 4% -> 13% of each run, Pallas kernels for 0% -> 26%
where the time goes in v1:
time: 323 us; the launch traced here: 316 us
  Pallas kernels  115 us (36%)
  waiting for transfers between devices  86.3 us (27%)
  starting transfers between devices  69.9 us (22%)
  local copies, waits for them, and re-layouts  30.7 us (10%)
  other arithmetic  13 us (4%)
    ppermute x71, waiting for transfers between devices, swap(): return lax.ppermute(value, axis, [(i, i ^ bit) for i in range(count)])  86.3 us
    ppermute x71, starting transfers between devices, swap(): return lax.ppermute(value, axis, [(i, i ^ bit) for i in range(count)])  69.9 us
    pallas_call x2, Pallas kernels, mid(): pl.pallas_call(functools.partial(mid_kernel, half, width), grid_spec=pltp...  60.8 us
    pallas_call x2, Pallas kernels, attn_bwd(): pl.pallas_call(functools.partial(attn_bwd_kernel, half, heads, short_bloc...  36 us
    pallas_call x2, Pallas kernels, attn_fwd(): pl.pallas_call(functools.partial(attn_fwd_kernel, half, heads, short_bloc...  18 us
  transfers between devices with their start and end apart: 71, of which 18 were waited for; matrix products, arithmetic and copies ran while one was open for 13% of the time, Pallas kernels for 26%

profile of v1, /device:TPU:0, one launch (start us, length us, event | category | flops | bytes accessed | tf_op | source)
XLA Modules:
  0.0 316.5 jit_solution(12543575037717540927)
XLA Ops:
  0.6 3.0 collective-permute-start.16
  3.7 2.5 constant_dynamic-slice_fusion.12
  9.9 9.0 %attn_fwd0.1 = (bf16[4,576,512]{2,1,0:T(8,128)(2,1)}, bf16[192,512]{1,0:T(8,128)(2,1)}, bf16[192,512]{1,0:T(8,128)(2,1)}, bf16[192,512]{1,0:T(8,128)(2,1)}, bf16...) custom-call(s32[1]{0:T(128)} %bitcast.me, s32[16]{0:T(128)} %lens_s.7, s32[4]{0:T(128)} %lens_l.7, bf16[192,4096]{1,0:T(8,128)(2,1)} %refs_0_.3, ...), custom_call_target="tpu_custom_call" | custom-call | tf_op jit(solution)/shard_map/attn_fwd0/pallas_call | solution.py:96
  23.6 3.6 %collective-permute-done.1.refs_2_ = bf16[192,512]{1,0:T(8,128)(2,1)S(1)} collective-permute-done((bf16[192,512]{1,0:T(8,128)(2,1)}, bf16[192,512]{1,0:T(8,128)(2,1)S(1)}, u32[]{:S(2)}, u32[]{:S(2)}) %collective-permute-start.1) | collective-permute-done | bytes 196640 | tf_op jit(solution)/shard_map/ppermute | solution.py:419
  27.2 3.1 collective-permute-done.2.refs_3_
  32.6 5.1 %collective-permute-done.10.refs_15_ = bf16[192,768]{1,0:T(8,128)(2,1)S(1)} collective-permute-done((bf16[192,768]{1,0:T(8,128)(2,1)S(1)}, bf16[192,768]{1,0:T(8,128)(2,1)S(1)}, u32[]{:S(2)}, u32[]{:S(2)}) %collective-permute-start.10) | collective-permute-done | bytes 294944 | tf_op jit(solution)/shard_map/ppermute | solution.py:419
  37.7 6.3 %collective-permute-done.13.refs_19_ = bf16[192,768]{1,0:T(8,128)(2,1)S(1)} collective-permute-done((bf16[192,768]{1,0:T(8,128)(2,1)S(1)}, bf16[192,768]{1,0:T(8,128)(2,1)S(1)}, u32[]{:S(2)}, u32[]{:S(2)}) %collective-permute-start.13) | collective-permute-done | bytes 294944 | tf_op jit(solution)/shard_map/ppermute | solution.py:419
  44.0 5.8 %collective-permute-done.7.refs_11_ = bf16[192,768]{1,0:T(8,128)(2,1)S(1)} collective-permute-done((bf16[192,768]{1,0:T(8,128)(2,1)S(1)}, bf16[192,768]{1,0:T(8,128)(2,1)S(1)}, u32[]{:S(2)}, u32[]{:S(2)}) %collective-permute-start.7) | collective-permute-done | bytes 294944 | tf_op jit(solution)/shard_map/ppermute | solution.py:419
  50.4 9.0 %attn_fwd1.1 = (bf16[4,576,512]{2,1,0:T(8,128)(2,1)}, bf16[192,512]{1,0:T(8,128)(2,1)}, bf16[192,512]{1,0:T(8,128)(2,1)}, bf16[192,512]{1,0:T(8,128)(2,1)}, bf16...) custom-call(s32[1]{0:T(128)} %bitcast.me, s32[16]{0:T(128)} %lens_s.7, s32[4]{0:T(128)} %lens_l.7, bf16[192,4096]{1,0:T(8,128)(2,1)} %refs_0_.3, ...), custom_call_target="tpu_custom_call" | custom-call | tf_op jit(solution)/shard_map/attn_fwd1/pallas_call | solution.py:96
  69.3 28.9 %mid0.1 = (bf16[512,768]{1,0:T(8,128)(2,1)}, bf16[192,512]{1,0:T(8,128)(2,1)}, bf16[192,512]{1,0:T(8,128)(2,1)}, bf16[192,512]{1,0:T(8,128)(2,1)}, bf16[192,512]...) custom-call(s32[1]{0:T(128)} %bitcast.me, ...), custom_call_target="tpu_custom_call" | custom-call | tf_op jit(solution)/shard_map/mid0/pallas_call | solution.py:388
  99.1 31.9 %mid1.1 = (bf16[512,768]{1,0:T(8,128)(2,1)}, bf16[192,512]{1,0:T(8,128)(2,1)}, bf16[192,512]{1,0:T(8,128)(2,1)}, bf16[192,512]{1,0:T(8,128)(2,1)}, bf16[192,512]...) custom-call(s32[1]{0:T(128)} %bitcast.me, ...), custom_call_target="tpu_custom_call" | custom-call | tf_op jit(solution)/shard_map/mid1/pallas_call | solution.py:388
  132.6 10.4 %collective-permute-done.55 = f32[768,16]{1,0:T(8,128)S(1)} collective-permute-done((f32[768,16]{1,0:T(8,128)}, f32[768,16]{1,0:T(8,128)S(1)}, u32[]{:S(2)}, u32[]{:S(2)}) %collective-permute-start.55) | collective-permute-done | bytes 49184 | tf_op jit(solution)/shard_map/ppermute | solution.py:419
  145.7 9.3 %collective-permute-done.56 = f32[768,16]{1,0:T(8,128)S(1)} collective-permute-done((f32[768,16]{1,0:T(8,128)S(1)}, f32[768,16]{1,0:T(8,128)S(1)}, u32[]{:S(2)}, u32[]{:S(2)}) %collective-permute-start.56) | collective-permute-done | bytes 49184 | tf_op jit(solution)/shard_map/ppermute | solution.py:419
  155.1 2.7 collective-permute-start.57
  158.1 16.4 %collective-permute-done.57 = f32[768,16]{1,0:T(8,128)S(1)} collective-permute-done((f32[768,16]{1,0:T(8,128)S(1)}, f32[768,16]{1,0:T(8,128)S(1)}, u32[]{:S(2)}, u32[]{:S(2)}) %collective-permute-start.57) | collective-permute-done | bytes 49184 | tf_op jit(solution)/shard_map/ppermute | solution.py:419
  190.4 2.6 slice.91
  198.9 17.7 %attn_bwd0.1 = (f32[192,4096]{1,0:T(8,128)}, f32[576,192]{1,0:T(8,128)}, f32[576,1]{1,0:T(8,128)}) custom-call(s32[1]{0:T(128)} %bitcast.me, s32[16]{0:T(128)} %lens_s.7, s32[4]{0:T(128)} %lens_l.7, bf16[192,4096]{1,0:T(8,128)(2,1)} %refs_0_.3, bf16[192,576]{1,0:T(8,128)(2,1)} %bitcast.98, bf16[4,576,512]{2,1,0:T(8,128)(2,1)} %get-tuple-element.82.refs_2_, ...), custom_call_target="tpu_custom_call" | custom-call | tf_op jit(solution)/shard_map/attn_bwd0/pallas_call | solution.py:223
  219.6 18.3 %attn_bwd1.1 = (f32[192,4096]{1,0:T(8,128)}, f32[576,192]{1,0:T(8,128)}, f32[576,1]{1,0:T(8,128)}) custom-call(s32[1]{0:T(128)} %bitcast.me, s32[16]{0:T(128)} %lens_s.7, s32[4]{0:T(128)} %lens_l.7, bf16[192,4096]{1,0:T(8,128)(2,1)} %refs_0_.3, bf16[192,576]{1,0:T(8,128)(2,1)} %bitcast.99, ...), custom_call_target="tpu_custom_call", output_to_operand_aliasing={{0}: (17, {})} | custom-call | tf_op jit(solution)/shard_map/attn_bwd1/pallas_call | solution.py:223
  253.7 2.9 collective-permute-start.39
  270.9 6.2 %collective-permute-done.59 = f32[768,16]{1,0:T(8,128)S(1)} collective-permute-done((f32[768,16]{1,0:T(8,128)S(1)}, f32[768,16]{1,0:T(8,128)S(1)}, u32[]{:S(2)}, u32[]{:S(2)}) %collective-permute-start.59) | collective-permute-done | bytes 49184 | tf_op jit(solution)/shard_map/ppermute | solution.py:419
  277.1 8.4 %collective-permute-done.47 = bf16[768,192]{1,0:T(8,128)(2,1)S(1)} collective-permute-done((bf16[768,192]{1,0:T(8,128)(2,1)S(1)}, bf16[768,192]{1,0:T(8,128)(2,1)S(1)}, u32[]{:S(2)}, u32[]{:S(2)}) %collective-permute-start.47) | collective-permute-done | bytes 294944 | tf_op jit(solution)/shard_map/ppermute | solution.py:419
  291.3 3.0 collective-permute-done.61
  308.4 2.7 collective-permute-start.68
  313.0 2.5 collective-permute-done.68
  (288 shorter events, 103.7 us)
Async XLA Ops:
  21.4 22.6 %collective-permute-start.13 = (bf16[192,768]{1,0:T(8,128)(2,1)S(1)}, bf16[192,768]{1,0:T(8,128)(2,1)S(1)}, u32[]{:S(2)}, u32[]{:S(2)}) collective-permute-start(bf16[192,768]{1,0:T(8,128)(2,1)S(1)} %copy-done.4), channel_id=1, source_target_pairs={{0,2},{1,3},{2,0},{3,1},{4,6},{5,7},{6,4},{7,5},{8,10},{9,11},{10,... | collective-permute-start | bytes 884744 | tf_op jit(solution)/shard_map/ppermute | solution.py:419
  23.2 26.6 %collective-permute-start.7 = (bf16[192,768]{1,0:T(8,128)(2,1)S(1)}, bf16[192,768]{1,0:T(8,128)(2,1)S(1)}, u32[]{:S(2)}, u32[]{:S(2)}) collective-permute-start(bf16[192,768]{1,0:T(8,128)(2,1)S(1)} %copy-done.2), channel_id=1, source_target_pairs={{0,2},{1,3},{2,0},{3,1},{4,6},{5,7},{6,4},{7,5},{8,10},{9,11},{10,... | collective-permute-start | bytes 884744 | tf_op jit(solution)/shard_map/ppermute | solution.py:419
  27.2 22.6 %collective-permute-start.12 = (bf16[192,768]{1,0:T(8,128)(2,1)S(1)}, bf16[192,768]{1,0:T(8,128)(2,1)S(1)}, u32[]{:S(2)}, u32[]{:S(2)}) collective-permute-start(bf16[192,768]{1,0:T(8,128)(2,1)S(1)} %copy-done.4), channel_id=1, source_target_pairs={{0,1},{1,0},{2,3},{3,2},{4,5},{5,4},{6,7},{7,6},{8,9},{9,8},{10,11... | collective-permute-start | bytes 884744 | tf_op jit(solution)/shard_map/ppermute | solution.py:419
  32.3 27.1 %collective-permute-start.6 = (bf16[192,768]{1,0:T(8,128)(2,1)S(1)}, bf16[192,768]{1,0:T(8,128)(2,1)S(1)}, u32[]{:S(2)}, u32[]{:S(2)}) collective-permute-start(bf16[192,768]{1,0:T(8,128)(2,1)S(1)} %copy-done.2), channel_id=1, source_target_pairs={{0,1},{1,0},{2,3},{3,2},{4,5},{5,4},{6,7},{7,6},{8,9},{9,8},{10,11... | collective-permute-start | bytes 884744 | tf_op jit(solution)/shard_map/ppermute | solution.py:419
  37.7 22.1 %collective-permute-start.9 = (bf16[192,768]{1,0:T(8,128)(2,1)S(1)}, bf16[192,768]{1,0:T(8,128)(2,1)S(1)}, u32[]{:S(2)}, u32[]{:S(2)}) collective-permute-start(bf16[192,768]{1,0:T(8,128)(2,1)S(1)} %copy-done.3), channel_id=1, source_target_pairs={{0,1},{1,0},{2,3},{3,2},{4,5},{5,4},{6,7},{7,6},{8,9},{9,8},{10,11... | collective-permute-start | bytes 884744 | tf_op jit(solution)/shard_map/ppermute | solution.py:419
  44.0 16.9 %collective-permute-start.11 = (bf16[192,768]{1,0:T(8,128)(2,1)S(1)}, bf16[192,768]{1,0:T(8,128)(2,1)S(1)}, u32[]{:S(2)}, u32[]{:S(2)}) collective-permute-start(bf16[192,768]{1,0:T(8,128)(2,1)S(1)} %collective-permute-done.10.refs_15_), channel_id=1, source_target_pairs={{0,1},{1,0},{2,3},{3,2},{4,5},{5,4},{6,7},{7,6},{8,9},{9,8},{10,11... | collective-permute-start | bytes 884744 | tf_op jit(solution)/shard_map/ppermute | solution.py:419
  59.4 38.9 %collective-permute-start.22 = (bf16[192,512]{1,0:T(8,128)(2,1)}, bf16[192,512]{1,0:T(8,128)(2,1)S(1)}, u32[]{:S(2)}, u32[]{:S(2)}) collective-permute-start(bf16[192,512]{1,0:T(8,128)(2,1)} %get-tuple-element.110), channel_id=1, source_target_pairs={{0,2},{1,3},{2,0},{3,1},{4,6},{5,7},{6,4},{7,5},{8,10},{9,11},{10,... | collective-permute-start | bytes 589832 | tf_op jit(solution)/shard_map/ppermute | solution.py:419
  59.8 38.5 %collective-permute-start.23 = (bf16[192,512]{1,0:T(8,128)(2,1)}, bf16[192,512]{1,0:T(8,128)(2,1)S(1)}, u32[]{:S(2)}, u32[]{:S(2)}) collective-permute-start(bf16[192,512]{1,0:T(8,128)(2,1)} %get-tuple-element.109), channel_id=1, source_target_pairs={{0,3},{1,2},{2,1},{3,0},{4,7},{5,6},{6,5},{7,4},{8,11},{9,10},{10,... | collective-permute-start | bytes 589832 | tf_op jit(solution)/shard_map/ppermute | solution.py:419
  60.9 37.4 %collective-permute-start.18 = (bf16[192,512]{1,0:T(8,128)(2,1)}, bf16[192,512]{1,0:T(8,128)(2,1)S(1)}, u32[]{:S(2)}, u32[]{:S(2)}) collective-permute-start(bf16[192,512]{1,0:T(8,128)(2,1)} %get-tuple-element.64), channel_id=1, source_target_pairs={{0,1},{1,0},{2,3},{3,2},{4,5},{5,4},{6,7},{7,6},{8,9},{9,8},{10,11... | collective-permute-start | bytes 589832 | tf_op jit(solution)/shard_map/ppermute | solution.py:419
  61.7 36.7 %collective-permute-start.19 = (bf16[192,512]{1,0:T(8,128)(2,1)}, bf16[192,512]{1,0:T(8,128)(2,1)}, u32[]{:S(2)}, u32[]{:S(2)}) collective-permute-start(bf16[192,512]{1,0:T(8,128)(2,1)} %get-tuple-element.65), channel_id=1, source_target_pairs={{0,2},{1,3},{2,0},{3,1},{4,6},{5,7},{6,4},{7,5},{8,10},{9,11},{10,... | collective-permute-start | bytes 589832 | tf_op jit(solution)/shard_map/ppermute | solution.py:419
  61.9 36.4 %collective-permute-start.20 = (bf16[192,512]{1,0:T(8,128)(2,1)}, bf16[192,512]{1,0:T(8,128)(2,1)}, u32[]{:S(2)}, u32[]{:S(2)}) collective-permute-start(bf16[192,512]{1,0:T(8,128)(2,1)} %get-tuple-element.66), channel_id=1, source_target_pairs={{0,3},{1,2},{2,1},{3,0},{4,7},{5,6},{6,5},{7,4},{8,11},{9,10},{10,... | collective-permute-start | bytes 589832 | tf_op jit(solution)/shard_map/ppermute | solution.py:419
  155.1 19.4 %collective-permute-start.57 = (f32[768,16]{1,0:T(8,128)S(1)}, f32[768,16]{1,0:T(8,128)S(1)}, u32[]{:S(2)}, u32[]{:S(2)}) collective-permute-start(f32[768,16]{1,0:T(8,128)S(1)} %add.238), channel_id=1, source_target_pairs={{0,16},{4,20},{8,24},{12,28},{16,0},{20,4},{24,8},{28,12},{1,17},{... | collective-permute-start | bytes 147464 | tf_op jit(solution)/shard_map/ppermute | solution.py:419
  157.7 25.0 %collective-permute-start.30 = (bf16[192,512]{1,0:T(8,128)(2,1)}, bf16[192,512]{1,0:T(8,128)(2,1)}, u32[]{:S(2)}, u32[]{:S(2)}) collective-permute-start(bf16[192,512]{1,0:T(8,128)(2,1)} %get-tuple-element.85), channel_id=1, source_target_pairs={{0,1},{1,0},{2,3},{3,2},{4,5},{5,4},{6,7},{7,6},{8,9},{9,8},{10,11... | collective-permute-start | bytes 589832 | tf_op jit(solution)/shard_map/ppermute | solution.py:419
  157.7 25.1 %collective-permute-start.31 = (bf16[192,512]{1,0:T(8,128)(2,1)}, bf16[192,512]{1,0:T(8,128)(2,1)}, u32[]{:S(2)}, u32[]{:S(2)}) collective-permute-start(bf16[192,512]{1,0:T(8,128)(2,1)} %get-tuple-element.86), channel_id=1, source_target_pairs={{0,2},{1,3},{2,0},{3,1},{4,6},{5,7},{6,4},{7,5},{8,10},{9,11},{10,... | collective-permute-start | bytes 589832 | tf_op jit(solution)/shard_map/ppermute | solution.py:419
  194.4 22.1 %collective-permute-start.25 = (bf16[192,512]{1,0:T(8,128)(2,1)}, bf16[192,512]{1,0:T(8,128)(2,1)S(1)}, u32[]{:S(2)}, u32[]{:S(2)}) collective-permute-start(bf16[192,512]{1,0:T(8,128)(2,1)} %get-tuple-element.76), channel_id=1, source_target_pairs={{0,2},{1,3},{2,0},{3,1},{4,6},{5,7},{6,4},{7,5},{8,10},{9,11},{10,... | collective-permute-start | bytes 589832 | tf_op jit(solution)/shard_map/ppermute | solution.py:419
  196.1 21.0 %collective-permute-start.26 = (bf16[192,512]{1,0:T(8,128)(2,1)}, bf16[192,512]{1,0:T(8,128)(2,1)S(1)}, u32[]{:S(2)}, u32[]{:S(2)}) collective-permute-start(bf16[192,512]{1,0:T(8,128)(2,1)} %get-tuple-element.77), channel_id=1, source_target_pairs={{0,3},{1,2},{2,1},{3,0},{4,7},{5,6},{6,5},{7,4},{8,11},{9,10},{10,... | collective-permute-start | bytes 589832 | tf_op jit(solution)/shard_map/ppermute | solution.py:419
  196.1 21.1 %collective-permute-start.27 = (bf16[192,512]{1,0:T(8,128)(2,1)S(1)}, bf16[192,512]{1,0:T(8,128)(2,1)S(1)}, u32[]{:S(2)}, u32[]{:S(2)}) collective-permute-start(bf16[192,512]{1,0:T(8,128)(2,1)S(1)} %copy-done.43), channel_id=1, source_target_pairs={{0,1},{1,0},{2,3},{3,2},{4,5},{5,4},{6,7},{7,6},{8,9},{9,8},{10,11... | collective-permute-start | bytes 589832 | tf_op jit(solution)/shard_map/ppermute | solution.py:419
  196.6 22.2 %collective-permute-start.28 = (bf16[192,512]{1,0:T(8,128)(2,1)S(1)}, bf16[192,512]{1,0:T(8,128)(2,1)S(1)}, u32[]{:S(2)}, u32[]{:S(2)}) collective-permute-start(bf16[192,512]{1,0:T(8,128)(2,1)S(1)} %copy-done.42), channel_id=1, source_target_pairs={{0,2},{1,3},{2,0},{3,1},{4,6},{5,7},{6,4},{7,5},{8,10},{9,11},{10,... | collective-permute-start | bytes 589832 | tf_op jit(solution)/shard_map/ppermute | solution.py:419
  198.3 20.6 %collective-permute-start.29 = (bf16[192,512]{1,0:T(8,128)(2,1)S(1)}, bf16[192,512]{1,0:T(8,128)(2,1)S(1)}, u32[]{:S(2)}, u32[]{:S(2)}) collective-permute-start(bf16[192,512]{1,0:T(8,128)(2,1)S(1)} %copy-done.41), channel_id=1, source_target_pairs={{0,3},{1,2},{2,1},{3,0},{4,7},{5,6},{6,5},{7,4},{8,11},{9,10},{10,... | collective-permute-start | bytes 589832 | tf_op jit(solution)/shard_map/ppermute | solution.py:419
  216.6 41.5 %collective-permute-start.60 = (bf16[2,192,1536]{2,1,0:T(8,128)(2,1)}, bf16[2,192,1536]{2,1,0:T(8,128)(2,1)}, u32[]{:S(2)}, u32[]{:S(2)}) collective-permute-start(bf16[2,192,1536]{2,1,0:T(8,128)(2,1)} %slice.91), channel_id=1, source_target_pairs={{0,1},{1,0},{2,3},{3,2},{4,5},{5,4},{6,7},{7,6},{8,9},{9,8},{10,11... | collective-permute-start | bytes 3538952 | tf_op jit(solution)/shard_map/ppermute | solution.py:419
  217.1 36.5 %collective-permute-start.46 = (bf16[2,768,192]{1,2,0:T(8,128)(2,1)}, bf16[2,768,192]{1,2,0:T(8,128)(2,1)}, u32[]{:S(2)}, u32[]{:S(2)}) collective-permute-start(bf16[2,768,192]{1,2,0:T(8,128)(2,1)} %copy.69), channel_id=1, source_target_pairs={{0,1},{1,0},{2,3},{3,2},{4,5},{5,4},{6,7},{7,6},{8,9},{9,8},{10,11... | collective-permute-start | bytes 1769480 | tf_op jit(solution)/shard_map/ppermute | solution.py:419
  217.2 26.2 %collective-permute-start.70 = (f32[192,4]{0,1:T(4,128)}, f32[192,4]{0,1:T(4,128)S(1)}, u32[]{:S(2)}, u32[]{:S(2)}) collective-permute-start(f32[192,4]{0,1:T(4,128)} %slice_bitcast_fusion.4), channel_id=1, source_target_pairs={{0,2},{1,3},{2,0},{3,1},{4,6},{5,7},{6,4},{7,5},{8,10},{9,11},{10,... | collective-permute-start | bytes 9224 | tf_op jit(solution)/shard_map/ppermute | solution.py:419
  265.5 20.0 %collective-permute-start.47 = (bf16[768,192]{1,0:T(8,128)(2,1)S(1)}, bf16[768,192]{1,0:T(8,128)(2,1)S(1)}, u32[]{:S(2)}, u32[]{:S(2)}) collective-permute-start(bf16[768,192]{1,0:T(8,128)(2,1)S(1)} %slice_bitcast_fusion.2), channel_id=1, source_target_pairs={{0,2},{1,3},{2,0},{3,1},{4,6},{5,7},{6,4},{7,5},{8,10},{9,11},{10,... | collective-permute-start | bytes 884744 | tf_op jit(solution)/shard_map/ppermute | solution.py:419
  267.1 27.2 %collective-permute-start.61 = (bf16[192,1536]{1,0:T(8,128)(2,1)S(1)}, bf16[192,1536]{1,0:T(8,128)(2,1)S(1)}, u32[]{:S(2)}, u32[]{:S(2)}) collective-permute-start(bf16[192,1536]{1,0:T(8,128)(2,1)S(1)} %slice_bitcast_fusion), channel_id=1, source_target_pairs={{0,2},{1,3},{2,0},{3,1},{4,6},{5,7},{6,4},{7,5},{8,10},{9,11},{10,... | collective-permute-start | bytes 1769480 | tf_op jit(solution)/shard_map/ppermute | solution.py:419
  (91 other events, 1066.2 us)
